TPU v7x, 32 devices: a whole 2x2x4 slice. The times are simulated.
32 devices in a mesh: frame: 4 (over z), space: 8 (over y, x, core).
Axes of the slice: x: 2, y: 2, z: 4, core: 2. Of those that a mesh axis runs over, the one named last changes fastest.
Arguments:
- latents: bfloat16 [2, 4, 512, 3072], P(None, 'frame', 'space'), may hold values from -6 to 6
- target: bfloat16 [2, 4, 512, 3072], P(None, 'frame', 'space'), may hold values from -6 to 6
- timesteps: int32 [2], replicated, may hold values from 0 to 999
- valid: int32 [2, 2], replicated, may hold values from 1 to 16, as said below
- tile_mask: int32 [2, 16, 16], replicated, may hold values from 0 to 1, as said below
- w_mod: bfloat16 [256, 18432], replicated, may hold values from -0.5 to 0.5
- w_sqkv: bfloat16 [3, 3072, 2048], P(None, None, 'space'), may hold values from -0.109375 to 0.109375
- w_sout: bfloat16 [2048, 3072], P('space'), may hold values from -0.125 to 0.125
- w_tqkv: bfloat16 [3, 3072, 2048], P(None, None, 'frame'), may hold values from -0.109375 to 0.109375
- w_tout: bfloat16 [2048, 3072], P('frame'), may hold values from -0.125 to 0.125
Outputs:
- mixed: bfloat16 [2, 4, 512, 3072], P(None, 'frame', 'space')
- loss: float32 [], replicated
Inputs may be any that keep to these rules, and one draw needn't show every extreme that they name: Each video's valid frame count is 1 to 4 and valid tile count 1 to 16; video 0 is whole. `tile_mask`: entries are 0 or 1, with ones on the diagonal of every video's mask.
All inputs are finite; a program needn't handle non-finite values.
Results may differ from a plain program's by a relative error of at most 0.017.
Values may be sent and summed in bfloat16 or wider, within the bound.
A program may use at most 128 MiB of HBM per device.

v0:
```python
import math
import jax
import jax.numpy as jnp
from jax import lax
from jax.sharding import PartitionSpec as P

HEAD_DIM = 128
FREQ = 256
TILE = 32


def layer_norm(values):
    mean = jnp.mean(values, -1, keepdims=True)
    centred = values - mean
    var = jnp.mean(centred * centred, -1, keepdims=True)
    return centred * lax.rsqrt(var + 1e-06)


def time_embed(timesteps):
    half = FREQ // 2
    freqs = jnp.exp(-math.log(10000.0) * jnp.arange(half, dtype=jnp.float32) / half)
    angles = timesteps.astype(jnp.float32)[:, None] * freqs[None, :]
    return jnp.concatenate([jnp.cos(angles), jnp.sin(angles)], -1).astype(jnp.bfloat16)


def modulate(values, shift, scale):
    return (
        layer_norm(values.astype(jnp.float32)) * (1.0 + scale[:, None, None, :])
        + shift[:, None, None, :]
    ).astype(jnp.bfloat16)


def frame_attention(qkv, count, tiles, heads):
    length = qkv.shape[0]
    cols = heads * HEAD_DIM
    scale = 1.0 / math.sqrt(HEAD_DIM)
    query = jnp.transpose(qkv[:, :cols].reshape(length, heads, HEAD_DIM), (1, 0, 2))
    keys = jnp.transpose(qkv[:, cols : 2 * cols].reshape(length, heads, HEAD_DIM), (1, 0, 2))
    values = jnp.transpose(qkv[:, 2 * cols :].reshape(length, heads, HEAD_DIM), (1, 0, 2))
    tile_ids = jnp.arange(length, dtype=jnp.int32) // TILE
    expanded = jnp.repeat(jnp.repeat(tiles, TILE, axis=0), TILE, axis=1)
    allowed = (expanded == 1) & (tile_ids[None, :] < count) | (
        tile_ids[:, None] == tile_ids[None, :]
    )

    def one_head(parts):
        q_head, k_head, v_head = parts
        scores = (
            lax.dot_general(
                q_head, k_head, (((1,), (1,)), ((), ())), preferred_element_type=jnp.float32
            )
            * scale
        )
        scores = jnp.where(allowed, scores, -1e30)
        top = jnp.max(scores, -1, keepdims=True)
        weights = jnp.exp(scores - top)
        probs = (weights / jnp.sum(weights, -1, keepdims=True)).astype(jnp.bfloat16)
        return jnp.dot(probs, v_head, preferred_element_type=jnp.float32).astype(jnp.bfloat16)

    outs = lax.map(one_head, (query, keys, values))
    return jnp.transpose(outs, (1, 0, 2)).reshape(length, cols)


def temporal_attention(qkv, count, heads):
    frames, places = (qkv.shape[0], qkv.shape[1])
    cols = heads * HEAD_DIM
    scale = 1.0 / math.sqrt(HEAD_DIM)
    query = qkv[..., :cols].reshape(frames, places, heads, HEAD_DIM)
    keys = qkv[..., cols : 2 * cols].reshape(frames, places, heads, HEAD_DIM)
    values = qkv[..., 2 * cols :].reshape(frames, places, heads, HEAD_DIM)
    scores = jnp.einsum("fphd,gphd->phfg", query, keys, preferred_element_type=jnp.float32) * scale
    frame_ids = jnp.arange(frames, dtype=jnp.int32)
    allowed = (frame_ids[None, :] < count) | (frame_ids[:, None] == frame_ids[None, :])
    scores = jnp.where(allowed, scores, -1e30)
    top = jnp.max(scores, -1, keepdims=True)
    weights = jnp.exp(scores - top)
    probs = (weights / jnp.sum(weights, -1, keepdims=True)).astype(jnp.bfloat16)
    outs = jnp.einsum("phfg,gphd->fphd", probs, values, preferred_element_type=jnp.float32).astype(
        jnp.bfloat16
    )
    return outs.reshape(frames, places, cols)


def group_project(attended, w_out, groups):
    rows = attended.shape[0]
    width = w_out.shape[1]
    parts = attended.reshape(rows, groups, -1)
    weights = w_out.reshape(groups, -1, width)
    terms = jnp.einsum("rgc,gcd->rgd", parts, weights, preferred_element_type=jnp.float32).astype(
        jnp.bfloat16
    )
    return jnp.sum(terms.astype(jnp.float32), axis=1)


def shards(latents, target, timesteps, valid, tile_mask, w_mod, w_sqkv, w_sout, w_tqkv, w_tout):
    videos, frames_dev, span_dev, width = latents.shape
    space_count = lax.axis_size("space")
    frame_count = lax.axis_size("frame")
    embed = time_embed(timesteps)
    mod = jnp.dot(embed, w_mod, preferred_element_type=jnp.float32)
    shift_one, scale_one, gate_one, shift_two, scale_two, gate_two = jnp.split(mod, 6, axis=1)
    h_one = modulate(latents, shift_one, scale_one)
    spatial_heads = w_sqkv.shape[2] // HEAD_DIM
    w_flat = jnp.concatenate([w_sqkv[0], w_sqkv[1], w_sqkv[2]], axis=1)
    qkv_space = jnp.dot(
        lax.all_gather(h_one, "space", axis=2, tiled=True),
        w_flat,
        preferred_element_type=jnp.float32,
    ).astype(jnp.bfloat16)
    span = qkv_space.shape[2]
    frames_flat = qkv_space.reshape(videos * frames_dev, span, -1)
    tile_counts = jnp.repeat(valid[:, 1], frames_dev)
    tiles = jnp.repeat(tile_mask, frames_dev, axis=0)

    def per_frame(parts):
        frame_qkv, count, tiles_one = parts
        return frame_attention(frame_qkv, count, tiles_one, spatial_heads)

    spatial_att = lax.map(per_frame, (frames_flat, tile_counts, tiles)).reshape(
        videos, frames_dev, span, -1
    )
    spatial_att = jnp.transpose(spatial_att, (2, 0, 1, 3))
    w_sall = lax.all_gather(w_sout, "space", axis=0, tiled=True)
    own_rows = lax.all_to_all(spatial_att, "space", split_axis=0, concat_axis=3, tiled=True)
    spatial = group_project(
        own_rows.reshape(span_dev * videos * frames_dev, -1), w_sall, space_count
    )
    spatial = spatial.reshape(span_dev, videos, frames_dev, width)
    spatial = jnp.transpose(spatial, (1, 2, 0, 3))
    x_one = (latents.astype(jnp.float32) + gate_one[:, None, None, :] * spatial).astype(
        jnp.bfloat16
    )
    h_two = modulate(x_one, shift_two, scale_two)
    temporal_heads = w_tqkv.shape[2] // HEAD_DIM
    w_tflat = jnp.concatenate([w_tqkv[0], w_tqkv[1], w_tqkv[2]], axis=1)
    qkv_frame = jnp.dot(
        lax.all_gather(h_two, "frame", axis=1, tiled=True),
        w_tflat,
        preferred_element_type=jnp.float32,
    ).astype(jnp.bfloat16)

    def per_video(parts):
        video_qkv, count = parts
        return temporal_attention(video_qkv, count, temporal_heads)

    temporal_att = lax.map(per_video, (qkv_frame, valid[:, 0]))
    temporal_att = jnp.transpose(temporal_att, (1, 0, 2, 3))
    w_tall = lax.all_gather(w_tout, "frame", axis=0, tiled=True)
    own_frames = lax.all_to_all(temporal_att, "frame", split_axis=0, concat_axis=3, tiled=True)
    temporal = group_project(
        own_frames.reshape(frames_dev * videos * span_dev, -1), w_tall, frame_count
    )
    temporal = temporal.reshape(frames_dev, videos, span_dev, width)
    temporal = jnp.transpose(temporal, (1, 0, 2, 3))
    mixed = (x_one.astype(jnp.float32) + gate_two[:, None, None, :] * temporal).astype(jnp.bfloat16)
    diff = mixed.astype(jnp.float32) - target.astype(jnp.float32)
    squares = jnp.mean(diff * diff, -1)
    frame_ids = lax.axis_index("frame") * frames_dev + jnp.arange(frames_dev, dtype=jnp.int32)
    tile_ids = (lax.axis_index("space") * span_dev + jnp.arange(span_dev, dtype=jnp.int32)) // TILE
    mask = (frame_ids[None, :, None] < valid[:, 0][:, None, None]) & (
        tile_ids[None, None, :] < valid[:, 1][:, None, None]
    )
    local_total = jnp.sum(jnp.where(mask, squares, 0.0))
    total = lax.psum(local_total, ("frame", "space"))
    count = jnp.sum(valid[:, 0] * valid[:, 1]).astype(jnp.float32) * TILE
    return (mixed, total / count)


def solution(mesh):
    return jax.shard_map(
        shards,
        mesh=mesh,
        in_specs=(
            P(None, "frame", "space", None),
            P(None, "frame", "space", None),
            P(),
            P(),
            P(),
            P(),
            P(None, None, "space"),
            P("space", None),
            P(None, None, "frame"),
            P("frame", None),
        ),
        out_specs=(P(None, "frame", "space", None), P()),
        check_vma=False,
    )
```

profile of v0, /device:TPU:12, one launch (start us, length us, event | category | flops | bytes accessed | tf_op | source)
XLA Modules:
  0.0 503.2 jit_solution(8383597021539726154)
XLA Ops:
  7.2 0.7 convert_element_type.72
  8.0 5.1 %fusion.68 = f32[2,18432]{1,0:T(2,128)S(1)} fusion(bf16[256,18432]{1,0:T(8,128)(2,1)} %param.21, bf16[2,128]{1,0:T(2,128)(2,1)S(1)} %get-tuple-element.260, bf16[2,128]{1,0:T(2,128)(2,1)S(1)} %get-tuple-element.259), kind=kOutput, calls=%fused_computation.113 | convolution fusion | flops 18876416 | bytes 9585664 | tf_op jit(solution)/shard_map/dot_general | solution.py:100
  13.3 0.4 fusion.59
  13.7 1.3 fusion.62
  15.1 0.7 all-gather.7.cloned.1.call-update
  16.0 4.4 slice_bitcast_fusion.5
  20.4 41.2 %all-gather.5.cloned.1.call-done = bf16[2,1,512,3072]{3,2,0,1:T(8,128)(2,1)} async-done(((bf16[2,1,64,3072]{3,2,0,1:T(8,128)(2,1)}), bf16[2,1,512,3072]{3,2,0,1:T(8,128)(2,1)}) %all-gather.5.cloned.1.call-update) | async-done | bytes 6291472 | tf_op jit(solution)/shard_map/all_gather | solution.py:106
  61.6 9.9 %fusion.52 = bf16[2,512,768]{2,1,0:T(8,128)(2,1)} fusion(bf16[3072,256]{1,0:T(8,128)(2,1)} %get-tuple-element.251, bf16[3072,256]{1,0:T(8,128)(2,1)} %get-tuple-element.252, bf16[3072,256]{1,0:T(8,128)(2,1)S(1)} %get-tuple-element.250, bf16[2,1,512,3072]{3,2,0,1:T(8,128)(2,1)} %all-gather.5.cloned.1.call-done), kind=kOutput, calls=%fused_computation.84 | convolution fusion | flops 4846780416 | bytes 12582912 | tf_op jit(solution)/shard_map/dot_general | solution.py:105
  71.4 12.7 %while.43 = (s32[]{:T(128)}, bf16[2,512,256]{2,1,0:T(8,128)(2,1)S(1)}, bf16[2,512,768]{2,1,0:T(8,128)(2,1)}, s32[2,16,16]{2,1,0:T(8,128)S(1)}, s32[2]{0:T(128)S(1)}, /*index=5*/s32[]{:T(128)}, s32[]{:T(128)}, s32[]{:T(128)}) while((s32[]{:T(128)}, bf16[2,512,256]{2,1,0:T(8,128)(2,1)S(1)}, bf16[2,512,768]{2,1,0:T(8,128)(2,1)}, ...), condition=%wide.region_7.8_spmd, body=%wide.region_2.7_spmd.sunk | while | flops 137174784 | bytes 10541854 | solution.py:119
  71.4 1.3 constant_dynamic-slice_fusion.4
  73.4 0.6 dynamic_slice.70
  74.0 0.7 broadcast_compare_fusion.3
  74.7 2.7 while.45
  74.7 0.3 fusion.114
  75.0 0.4 fusion.115
  75.6 0.4 fusion.117
  76.1 0.3 fusion.114
  76.3 0.4 fusion.115
  76.9 0.4 fusion.117
  77.9 1.2 constant_dynamic-slice_fusion.4
  79.7 0.6 dynamic_slice.70
  80.3 0.7 broadcast_compare_fusion.3
  81.0 2.7 while.45
  81.0 0.3 fusion.114
  81.3 0.4 fusion.115
  81.9 0.4 fusion.117
  82.6 0.4 fusion.115
  83.2 0.4 fusion.117
  84.2 0.5 copy.99
  84.7 12.6 %all_to_all.30 = bf16[512,2,1,256]{3,1,2,0:T(2,128)(2,1)S(1)} all-to-all(bf16[512,2,1,256]{3,1,2,0:T(2,128)(2,1)S(1)} %bitcast.158), channel_id=1, replica_groups=mesh['frame'=4,'space'=8] {'space'}, dimensions={0} | all-to-all | bytes 1048576 | tf_op jit(solution)/shard_map/all_to_all | solution.py:124
  97.5 42.3 %all-gather.7.cloned.1.call-done = bf16[2048,3072]{1,0:T(8,128)(2,1)} async-done(((bf16[256,3072]{1,0:T(8,128)(2,1)}), bf16[2048,3072]{1,0:T(8,128)(2,1)}) %all-gather.7.cloned.1.call-update) | async-done | bytes 12582928 | tf_op jit(solution)/shard_map/all_gather | solution.py:123
  139.8 7.7 %convert_reduce_fusion = f32[128,3072]{1,0:T(8,128)} fusion(bf16[128,8,256]{2,0,1:T(8,128)(2,1)S(1)} %reshape_reshape.6, bf16[8,256,3072]{2,1,0:T(8,128)(2,1)} %bitcast.152), kind=kOutput, calls=%fused_computation.53 | convolution fusion | flops 1619656704 | bytes 14680064 | tf_op jit(solution)/shard_map/rgc,gcd->rgd/dot_general | solution.py:89
  147.5 2.2 reshape.315
  149.7 0.7 convert_reduce_fusion.2
  150.4 0.4 fusion.55
  150.8 1.3 fusion.58
  152.2 0.5 all-gather.11.cloned.1.call-update
  152.7 6.7 %slice_bitcast_fusion.2 = (bf16[3072,512]{1,0:T(8,128)(2,1)}, bf16[3072,512]{1,0:T(8,128)(2,1)}, bf16[3072,512]{1,0:T(8,128)(2,1)}) fusion(bf16[3,3072,512]{2,1,0:T(8,128)(2,1)} %param.24), kind=kLoop, calls=%fused_computation.72 | loop fusion | bytes 18874368 | tf_op jit(solution)/shard_map/squeeze | solution.py:135
  159.5 54.6 %all-gather.9.cloned.1.call-done = bf16[2,4,64,3072]{3,2,0,1:T(8,128)(2,1)} async-done(((bf16[2,1,64,3072]{3,2,0,1:T(8,128)(2,1)}), bf16[2,4,64,3072]{3,2,0,1:T(8,128)(2,1)}) %all-gather.9.cloned.1.call-update) | async-done | bytes 3145744 | tf_op jit(solution)/shard_map/all_gather | solution.py:137
  214.0 9.7 %fusion.45 = bf16[2,4,64,1536]{3,2,1,0:T(8,128)(2,1)S(1)} fusion(bf16[3072,512]{1,0:T(8,128)(2,1)} %get-tuple-element.248, bf16[3072,512]{1,0:T(8,128)(2,1)} %get-tuple-element.249, bf16[3072,512]{1,0:T(8,128)(2,1)} %get-tuple-element.247, bf16[2,4,64,3072]{3,2,0,1:T(8,128)(2,1)} %all-gather.9.cloned.1.call-done), kind=kOutput, calls=%fused_computation.73 | convolution fusion | flops 4860936192 | bytes 14155776 | tf_op jit(solution)/shard_map/dot_general | solution.py:136
  223.7 11.9 %while.44 = (s32[]{:T(128)}, bf16[2,4,64,512]{3,2,0,1:T(8,128)(2,1)}, bf16[2,4,64,1536]{3,2,1,0:T(8,128)(2,1)S(1)}, s32[2]{0:T(128)S(1)}, s32[]{:T(128)}) while((s32[]{:T(128)}, bf16[2,4,64,512]{3,2,0,1:T(8,128)(2,1)}, bf16[2,4,64,1536]{3,2,1,0:T(8,128)(2,1)S(1)}, s32[2]{0:T(128)S(1)}, s32[]{:T(128)}) %tuple.106), condition=%wide.region_14.15_spmd, body=%wide.region_11.14_spmd.sunk | while | flops 2252841 | bytes 7479929 | solution.py:146
  224.0 0.8 reshape.325
  224.7 1.4 fusion.109
  226.2 0.3 copy.115
  226.5 0.6 dynamic_slice.72
  227.1 0.7 iota_compare_fusion.3
  227.9 0.3 copy.116
  228.3 0.4 fusion.112
  228.9 0.7 bitcast_dynamic-update-slice_fusion.2
  229.9 0.8 reshape.325
  230.7 1.4 fusion.109
  232.1 0.3 copy.115
  232.4 0.6 dynamic_slice.72
  233.0 0.7 iota_compare_fusion.3
  233.8 0.3 copy.116
  234.2 0.4 fusion.112
  234.8 0.7 bitcast_dynamic-update-slice_fusion.2
  235.6 6.2 %all-to-all-start.1 = ((bf16[4,2,64,512]{3,2,1,0:T(8,128)(2,1)}), bf16[4,2,64,512]{3,2,1,0:T(8,128)(2,1)S(1)}, u32[]{:S(2)}, u32[]{:S(2)}) async-start(bf16[4,2,64,512]{3,2,1,0:T(8,128)(2,1)} %bitcast.161), calls=%async_computation.1 | async-start | bytes 1048576 | tf_op jit(solution)/shard_map/all_to_all | solution.py:149
  241.8 0.6 multiply_reduce_fusion.1
  243.1 198.7 %all-gather.11.cloned.1.call-done = bf16[2048,3072]{1,0:T(8,128)(2,1)} async-done(((bf16[512,3072]{1,0:T(8,128)(2,1)}), bf16[2048,3072]{1,0:T(8,128)(2,1)}) %all-gather.11.cloned.1.call-update) | async-done | bytes 12582928 | tf_op jit(solution)/shard_map/all_gather | solution.py:148
  441.8 6.6 %convert_reduce_fusion.1 = f32[128,3072]{1,0:T(8,128)S(1)} fusion(bf16[128,4,512]{2,0,1:T(8,128)(2,1)S(1)} %bitcast.157, bf16[4,512,3072]{2,1,0:T(8,128)(2,1)} %bitcast.153), kind=kOutput, calls=%fused_computation.62 | convolution fusion | flops 1614938112 | bytes 14680064 | tf_op jit(solution)/shard_map/rgc,gcd->rgd/dot_general | solution.py:89
  448.4 1.4 multiply_reduce_fusion
  449.8 0.7 fusion.67
  450.5 44.4 %psum.7 = f32[]{:T(128)} all-reduce(f32[]{:T(128)} %fusion.67), channel_id=1, replica_groups=mesh['frame'=4,'space'=8] {'frame','space'}, use_global_device_ids=true, to_apply=%region_18.19 | all-reduce | flops 1 | bytes 8 | tf_op jit(solution)/shard_map/psum | solution.py:164
  (76 shorter events, 5.5 us)
Async XLA Ops:
  7.2 54.4 %all-gather.5.cloned.1.call-start = ((), (), s32[]{:S(2)}) async-start(), calls=%async_computation.2 | async-start | bytes 7077888 | tf_op jit(solution)/shard_map/all_gather | solution.py:106
  8.0 5.1 %copy-start = (bf16[2,1,64,3072]{3,2,1,0:T(8,128)(2,1)S(1)}, bf16[2,1,64,3072]{3,2,1,0:T(8,128)(2,1)}, u32[]{:S(2)}) copy-start(bf16[2,1,64,3072]{3,2,1,0:T(8,128)(2,1)} %param.16) | copy-start | bytes 2359300
  15.0 0.8 copy-start.3
  15.0 124.8 %all-gather.7.cloned.1.call-start = ((), (), s32[]{:S(2)}) async-start(), calls=%async_computation.3 | async-start | bytes 14155776 | tf_op jit(solution)/shard_map/all_gather | solution.py:123
  15.8 198.3 %all-gather.9.cloned.1.call-start = ((), (), s32[]{:S(2)}) async-start(), calls=%async_computation.4 | async-start | bytes 3932160 | tf_op jit(solution)/shard_map/all_gather | solution.py:137
  61.6 9.9 %copy-start.2 = (s32[2,16,16]{2,1,0:T(8,128)S(1)}, s32[2,16,16]{2,1,0:T(8,128)}, u32[]{:S(2)}) copy-start(s32[2,16,16]{2,1,0:T(8,128)} %param.20) | copy-start | bytes 6148
  152.1 289.7 %all-gather.11.cloned.1.call-start = ((), (), s32[]{:S(2)}) async-start(), calls=%async_computation.5 | async-start | bytes 15728640 | tf_op jit(solution)/shard_map/all_gather | solution.py:148
  235.6 206.2 %all-to-all-start.1 = ((bf16[4,2,64,512]{3,2,1,0:T(8,128)(2,1)}), bf16[4,2,64,512]{3,2,1,0:T(8,128)(2,1)S(1)}, u32[]{:S(2)}, u32[]{:S(2)}) async-start(bf16[4,2,64,512]{3,2,1,0:T(8,128)(2,1)} %bitcast.161), calls=%async_computation.1 | async-start | bytes 1048576 | tf_op jit(solution)/shard_map/all_to_all | solution.py:149
  441.8 6.6 %copy-start.1 = (bf16[2,1,64,3072]{3,2,1,0:T(8,128)(2,1)S(1)}, bf16[2,1,64,3072]{3,2,1,0:T(8,128)(2,1)}, u32[]{:S(2)}) copy-start(bf16[2,1,64,3072]{3,2,1,0:T(8,128)(2,1)} %param.17) | copy-start | bytes 2359300
Sparse Core Ops, SparseCore 0:
  15.1 46.3 all-gather.4
  63.5 76.3 all-gather.6
  152.2 61.7 all-gather.8
  215.5 226.2 all-gather.10
where the time goes:
time: 504 us; the launch traced here: 503 us
  waiting for transfers between devices  338 us (67%)
  blocking collectives  57 us (11%)
  matrix products  45.9 us (9%)
  local copies, waits for them, and re-layouts  26.5 us (5%)
  between operations  16.3 us (3%)
  other arithmetic  12.6 us (2%)
  starting transfers between devices  6.4 us (1%)
    all_gather x1, waiting for transfers between devices, shards(): w_tall = lax.all_gather(w_tout, 'frame', axis=0, tiled=True)  199 us
    all_gather x1, waiting for transfers between devices, shards(): lax.all_gather(h_two, 'frame', axis=1, tiled=True)  54.6 us
    psum x1, blocking collectives, shards(): total = lax.psum(local_total, ('frame', 'space'))  44.4 us
    all_gather x1, waiting for transfers between devices, shards(): w_sall = lax.all_gather(w_sout, 'space', axis=0, tiled=True)  42.3 us
    all_gather x1, waiting for transfers between devices, shards(): lax.all_gather(h_one, 'space', axis=2, tiled=True)  41.2 us
    dot_general x2, matrix products, group_project(): jnp.einsum('rgc,gcd->rgd', parts, weights, preferred_element_type=jnp.flo...  14.3 us
    all_to_all x1, blocking collectives, shards(): lax.all_to_all(spatial_att, 'space', split_axis=0, concat_axis=3, tiled=T...  12.6 us
  transfers between devices with their start and end apart: 5, of which 4 were waited for; matrix products, arithmetic and copies ran while one was open for 11% of the time, Pallas kernels for 0%

commit v1 on v0

--- a/solution.py
+++ b/solution.py
@@ -121,7 +121,12 @@
     )
     spatial_att = jnp.transpose(spatial_att, (2, 0, 1, 3))
     w_sall = lax.all_gather(w_sout, "space", axis=0, tiled=True)
-    own_rows = lax.all_to_all(spatial_att, "space", split_axis=0, concat_axis=3, tiled=True)
+    own_rows = jnp.concatenate(
+        lax.all_to_all(
+            jnp.stack(jnp.split(spatial_att, lax.axis_size("space"), axis=0)), "space", 0, 0
+        ),
+        axis=3,
+    )
     spatial = group_project(
         own_rows.reshape(span_dev * videos * frames_dev, -1), w_sall, space_count
     )

time: 504 us -> 504 us (level)
  no operation moved by 1% of the time
where the time goes in v1:
time: 504 us
  waiting for transfers between devices  338 us (67%)
  blocking collectives  57.4 us (11%)
  matrix products  45.9 us (9%)
  local copies, waits for them, and re-layouts  26.6 us (5%)
  between operations  16.4 us (3%)
  other arithmetic  12.6 us (2%)
  starting transfers between devices  6.4 us (1%)
    all_gather x1, waiting for transfers between devices, shards(): w_tall = lax.all_gather(w_tout, 'frame', axis=0, tiled=True)  199 us
    all_gather x1, waiting for transfers between devices, shards(): lax.all_gather(h_two, 'frame', axis=1, tiled=True)  54.6 us
    psum x1, blocking collectives, shards(): total = lax.psum(local_total, ('frame', 'space'))  44.4 us
    all_gather x1, waiting for transfers between devices, shards(): w_sall = lax.all_gather(w_sout, 'space', axis=0, tiled=True)  42.2 us
    all_gather x1, waiting for transfers between devices, shards(): lax.all_gather(h_one, 'space', axis=2, tiled=True)  41.2 us
    dot_general x2, matrix products, group_project(): jnp.einsum('rgc,gcd->rgd', parts, weights, preferred_element_type=jnp.flo...  14.3 us
    all_to_all x1, blocking collectives, shards(): lax.all_to_all(jnp.stack(jnp.split(spatial_att, lax.axis_size('space'), a...  13 us
  transfers between devices with their start and end apart: 5, of which 4 were waited for; matrix products, arithmetic and copies ran while one was open for 11% of the time, Pallas kernels for 0%

profile of v1, /device:TPU:12, one launch (start us, length us, event | category | flops | bytes accessed | tf_op | source)
XLA Modules:
  0.0 503.6 jit_solution(8163191770682136042)
XLA Ops:
  7.2 0.7 convert_element_type.72
  8.0 5.1 %fusion.76 = f32[2,18432]{1,0:T(2,128)S(1)} fusion(bf16[256,18432]{1,0:T(8,128)(2,1)} %param.21, bf16[2,128]{1,0:T(2,128)(2,1)S(1)} %get-tuple-element.260, bf16[2,128]{1,0:T(2,128)(2,1)S(1)} %get-tuple-element.259), kind=kOutput, calls=%fused_computation.128 | convolution fusion | flops 18876416 | bytes 9585664 | tf_op jit(solution)/shard_map/dot_general | solution.py:100
  13.3 0.4 fusion.59
  13.7 1.3 fusion.62
  15.1 0.7 all-gather.7.cloned.1.call-update
  16.0 4.4 slice_bitcast_fusion.5
  20.4 41.2 %all-gather.5.cloned.1.call-done = bf16[2,1,512,3072]{3,2,0,1:T(8,128)(2,1)} async-done(((bf16[2,1,64,3072]{3,2,0,1:T(8,128)(2,1)}), bf16[2,1,512,3072]{3,2,0,1:T(8,128)(2,1)}) %all-gather.5.cloned.1.call-update) | async-done | bytes 6291472 | tf_op jit(solution)/shard_map/all_gather | solution.py:106
  61.6 9.9 %fusion.52 = bf16[2,512,768]{2,1,0:T(8,128)(2,1)} fusion(bf16[3072,256]{1,0:T(8,128)(2,1)} %get-tuple-element.251, bf16[3072,256]{1,0:T(8,128)(2,1)} %get-tuple-element.252, bf16[3072,256]{1,0:T(8,128)(2,1)S(1)} %get-tuple-element.250, bf16[2,1,512,3072]{3,2,0,1:T(8,128)(2,1)} %all-gather.5.cloned.1.call-done), kind=kOutput, calls=%fused_computation.84 | convolution fusion | flops 4846780416 | bytes 12582912 | tf_op jit(solution)/shard_map/dot_general | solution.py:105
  71.4 12.7 %while.43 = (s32[]{:T(128)}, bf16[2,512,256]{2,1,0:T(8,128)(2,1)S(1)}, bf16[2,512,768]{2,1,0:T(8,128)(2,1)}, s32[2,16,16]{2,1,0:T(8,128)S(1)}, s32[2]{0:T(128)S(1)}, /*index=5*/s32[]{:T(128)}, s32[]{:T(128)}, s32[]{:T(128)}) while((s32[]{:T(128)}, bf16[2,512,256]{2,1,0:T(8,128)(2,1)S(1)}, bf16[2,512,768]{2,1,0:T(8,128)(2,1)}, ...), condition=%wide.region_7.8_spmd, body=%wide.region_2.7_spmd.sunk | while | flops 137174784 | bytes 10541854 | solution.py:119
  71.4 1.3 constant_dynamic-slice_fusion.4
  73.4 0.6 dynamic_slice.70
  74.0 0.7 broadcast_compare_fusion.3
  74.7 2.7 while.45
  74.7 0.3 fusion.122
  75.0 0.4 fusion.123
  75.6 0.4 fusion.125
  76.1 0.3 fusion.122
  76.3 0.4 fusion.123
  76.9 0.4 fusion.125
  77.9 1.2 constant_dynamic-slice_fusion.4
  79.7 0.6 dynamic_slice.70
  80.3 0.7 broadcast_compare_fusion.3
  81.0 2.7 while.45
  81.0 0.3 fusion.122
  81.3 0.4 fusion.123
  81.9 0.4 fusion.125
  82.6 0.4 fusion.123
  83.2 0.4 fusion.125
  84.3 13.0 %all_to_all.20 = bf16[8,64,2,1,256]{4,1,2,3,0:T(8,128)(2,1)S(1)} all-to-all(bf16[8,64,2,1,256]{4,1,2,3,0:T(8,128)(2,1)S(1)} %fusion.65), channel_id=1, replica_groups=mesh['frame'=4,'space'=8] {'space'}, dimensions={0} | all-to-all | bytes 1048576 | tf_op jit(solution)/shard_map/all_to_all | solution.py:125
  97.3 0.5 copy.70
  98.0 42.2 %all-gather.7.cloned.1.call-done = bf16[2048,3072]{1,0:T(8,128)(2,1)} async-done(((bf16[256,3072]{1,0:T(8,128)(2,1)}), bf16[2048,3072]{1,0:T(8,128)(2,1)}) %all-gather.7.cloned.1.call-update) | async-done | bytes 12582928 | tf_op jit(solution)/shard_map/all_gather | solution.py:123
  140.3 7.7 %convert_reduce_fusion = f32[128,3072]{1,0:T(8,128)} fusion(bf16[128,8,256]{2,0,1:T(8,128)(2,1)S(1)} %reshape_reshape_reshape.3, bf16[8,256,3072]{2,1,0:T(8,128)(2,1)} %bitcast.180), kind=kOutput, calls=%fused_computation.53 | convolution fusion | flops 1619656704 | bytes 14680064 | tf_op jit(solution)/shard_map/rgc,gcd->rgd/dot_general | solution.py:89
  147.9 2.2 reshape.318
  150.2 0.7 convert_reduce_fusion.2
  150.9 0.4 fusion.55
  151.2 1.3 fusion.58
  152.6 0.5 all-gather.11.cloned.1.call-update
  153.1 6.7 %slice_bitcast_fusion.2 = (bf16[3072,512]{1,0:T(8,128)(2,1)}, bf16[3072,512]{1,0:T(8,128)(2,1)}, bf16[3072,512]{1,0:T(8,128)(2,1)}) fusion(bf16[3,3072,512]{2,1,0:T(8,128)(2,1)} %param.24), kind=kLoop, calls=%fused_computation.72 | loop fusion | bytes 18874368 | tf_op jit(solution)/shard_map/squeeze | solution.py:140
  159.9 54.6 %all-gather.9.cloned.1.call-done = bf16[2,4,64,3072]{3,2,0,1:T(8,128)(2,1)} async-done(((bf16[2,1,64,3072]{3,2,0,1:T(8,128)(2,1)}), bf16[2,4,64,3072]{3,2,0,1:T(8,128)(2,1)}) %all-gather.9.cloned.1.call-update) | async-done | bytes 3145744 | tf_op jit(solution)/shard_map/all_gather | solution.py:142
  214.5 9.7 %fusion.45 = bf16[2,4,64,1536]{3,2,1,0:T(8,128)(2,1)S(1)} fusion(bf16[3072,512]{1,0:T(8,128)(2,1)} %get-tuple-element.248, bf16[3072,512]{1,0:T(8,128)(2,1)} %get-tuple-element.249, bf16[3072,512]{1,0:T(8,128)(2,1)} %get-tuple-element.247, bf16[2,4,64,3072]{3,2,0,1:T(8,128)(2,1)} %all-gather.9.cloned.1.call-done), kind=kOutput, calls=%fused_computation.73 | convolution fusion | flops 4860936192 | bytes 14155776 | tf_op jit(solution)/shard_map/dot_general | solution.py:141
  224.1 11.9 %while.44 = (s32[]{:T(128)}, bf16[2,4,64,512]{3,2,0,1:T(8,128)(2,1)}, bf16[2,4,64,1536]{3,2,1,0:T(8,128)(2,1)S(1)}, s32[2]{0:T(128)S(1)}, s32[]{:T(128)}) while((s32[]{:T(128)}, bf16[2,4,64,512]{3,2,0,1:T(8,128)(2,1)}, bf16[2,4,64,1536]{3,2,1,0:T(8,128)(2,1)S(1)}, s32[2]{0:T(128)S(1)}, s32[]{:T(128)}) %tuple.106), condition=%wide.region_14.15_spmd, body=%wide.region_11.14_spmd.sunk | while | flops 2252841 | bytes 7479929 | solution.py:151
  224.4 0.8 reshape.328
  225.1 1.4 fusion.117
  226.6 0.3 copy.113
  226.9 0.6 dynamic_slice.72
  227.5 0.7 iota_compare_fusion.3
  228.3 0.3 copy.114
  228.7 0.4 fusion.120
  229.4 0.7 bitcast_dynamic-update-slice_fusion.2
  230.3 0.8 reshape.328
  231.1 1.4 fusion.117
  232.5 0.3 copy.113
  232.8 0.6 dynamic_slice.72
  233.4 0.7 iota_compare_fusion.3
  234.3 0.3 copy.114
  234.6 0.4 fusion.120
  235.3 0.7 bitcast_dynamic-update-slice_fusion.2
  236.0 6.2 %all-to-all-start.1 = ((bf16[4,2,64,512]{3,2,1,0:T(8,128)(2,1)}), bf16[4,2,64,512]{3,2,1,0:T(8,128)(2,1)S(1)}, u32[]{:S(2)}, u32[]{:S(2)}) async-start(bf16[4,2,64,512]{3,2,1,0:T(8,128)(2,1)} %bitcast.196), calls=%async_computation.1 | async-start | bytes 1048576 | tf_op jit(solution)/shard_map/all_to_all | solution.py:154
  242.3 0.6 multiply_reduce_fusion.1
  243.6 198.7 %all-gather.11.cloned.1.call-done = bf16[2048,3072]{1,0:T(8,128)(2,1)} async-done(((bf16[512,3072]{1,0:T(8,128)(2,1)}), bf16[2048,3072]{1,0:T(8,128)(2,1)}) %all-gather.11.cloned.1.call-update) | async-done | bytes 12582928 | tf_op jit(solution)/shard_map/all_gather | solution.py:153
  442.2 6.6 %convert_reduce_fusion.1 = f32[128,3072]{1,0:T(8,128)S(1)} fusion(bf16[128,4,512]{2,0,1:T(8,128)(2,1)S(1)} %bitcast.185, bf16[4,512,3072]{2,1,0:T(8,128)(2,1)} %bitcast.181), kind=kOutput, calls=%fused_computation.62 | convolution fusion | flops 1614938112 | bytes 14680064 | tf_op jit(solution)/shard_map/rgc,gcd->rgd/dot_general | solution.py:89
  448.9 1.4 multiply_reduce_fusion
  450.2 0.7 fusion.75
  450.9 44.4 %psum.7 = f32[]{:T(128)} all-reduce(f32[]{:T(128)} %fusion.75), channel_id=1, replica_groups=mesh['frame'=4,'space'=8] {'frame','space'}, use_global_device_ids=true, to_apply=%region_18.19 | all-reduce | flops 1 | bytes 8 | tf_op jit(solution)/shard_map/psum | solution.py:169
  (84 shorter events, 5.6 us)
Async XLA Ops:
  7.2 54.4 %all-gather.5.cloned.1.call-start = ((), (), s32[]{:S(2)}) async-start(), calls=%async_computation.2 | async-start | bytes 7077888 | tf_op jit(solution)/shard_map/all_gather | solution.py:106
  8.0 5.1 %copy-start = (bf16[2,1,64,3072]{3,2,1,0:T(8,128)(2,1)S(1)}, bf16[2,1,64,3072]{3,2,1,0:T(8,128)(2,1)}, u32[]{:S(2)}) copy-start(bf16[2,1,64,3072]{3,2,1,0:T(8,128)(2,1)} %param.16) | copy-start | bytes 2359300
  15.0 0.8 copy-start.3
  15.0 125.2 %all-gather.7.cloned.1.call-start = ((), (), s32[]{:S(2)}) async-start(), calls=%async_computation.3 | async-start | bytes 14155776 | tf_op jit(solution)/shard_map/all_gather | solution.py:123
  15.8 198.7 %all-gather.9.cloned.1.call-start = ((), (), s32[]{:S(2)}) async-start(), calls=%async_computation.4 | async-start | bytes 3932160 | tf_op jit(solution)/shard_map/all_gather | solution.py:142
  61.6 9.9 %copy-start.2 = (s32[2,16,16]{2,1,0:T(8,128)S(1)}, s32[2,16,16]{2,1,0:T(8,128)}, u32[]{:S(2)}) copy-start(s32[2,16,16]{2,1,0:T(8,128)} %param.20) | copy-start | bytes 6148
  152.6 289.7 %all-gather.11.cloned.1.call-start = ((), (), s32[]{:S(2)}) async-start(), calls=%async_computation.5 | async-start | bytes 15728640 | tf_op jit(solution)/shard_map/all_gather | solution.py:153
  236.0 206.2 %all-to-all-start.1 = ((bf16[4,2,64,512]{3,2,1,0:T(8,128)(2,1)}), bf16[4,2,64,512]{3,2,1,0:T(8,128)(2,1)S(1)}, u32[]{:S(2)}, u32[]{:S(2)}) async-start(bf16[4,2,64,512]{3,2,1,0:T(8,128)(2,1)} %bitcast.196), calls=%async_computation.1 | async-start | bytes 1048576 | tf_op jit(solution)/shard_map/all_to_all | solution.py:154
  442.2 6.6 %copy-start.1 = (bf16[2,1,64,3072]{3,2,1,0:T(8,128)(2,1)S(1)}, bf16[2,1,64,3072]{3,2,1,0:T(8,128)(2,1)}, u32[]{:S(2)}) copy-start(bf16[2,1,64,3072]{3,2,1,0:T(8,128)(2,1)} %param.17) | copy-start | bytes 2359300
Sparse Core Ops, SparseCore 0:
  15.1 46.3 all-gather.4
  63.5 76.7 all-gather.6
  152.7 61.7 all-gather.8
  215.9 226.3 all-gather.10
